TPU v7x, 32 devices: a whole 2x2x4 slice. The times are simulated.
32 devices in a mesh: section: 2 (over x), chan: 16 (over z, y, core).
Axes of the slice: x: 2, y: 2, z: 4, core: 2. Of those that a mesh axis runs over, the one named last changes fastest.
Arguments:
- raw_strain: float32 [1024, 20480], P('chan', 'section'), may hold values from -6 to 6
- seg_starts: int32 [16], P('section'), may hold values from 0 to 8192, as said below
- quality_mask: int32 [16, 1024], P(None, 'chan'), may hold values 0 or 1
- pair_reach: int32 [1024], P('chan'), may hold values from 224 to 448
Outputs:
- correlations: bfloat16 [1024, 102912], P('chan', 'section')
Inputs may be any that keep to these rules, and one draw needn't show every extreme that they name: `seg_starts`: segment k starts 1024 * (k mod 8) plus 0 to 1024 samples into its sub-window.
All inputs are finite; a program needn't handle non-finite values. No bound on the sum of `quality_mask` on one device may be relied on, other than what follows from the above.
Results may differ from a plain program's by a relative error of at most 0.0072.
Values may be sent and summed in bfloat16 or wider, within the bound.
A program may use at most 192 MiB of HBM per device.

v0:
```python
import math

import jax
import jax.numpy as jnp
from jax import lax
from jax.sharding import PartitionSpec as P

SEG = 2048
F = 1024
SMOOTH = 64
MAXLAG = 100
LAGS = 201
STOPS = 8


def from_behind(block, axis, distance):
    devices = range(lax.axis_size(axis))
    route = [(i - distance, i) for i in devices if i - distance in devices]
    return lax.ppermute(block, axis, route)


def hann_window():
    steps = jnp.arange(SEG, dtype=jnp.int32).astype(jnp.float32)
    return 0.5 - 0.5 * jnp.cos(2.0 * math.pi / SEG * steps)


def dft_rows():
    freqs = jnp.arange(F, dtype=jnp.int32)[:, None]
    times = jnp.arange(SEG, dtype=jnp.int32)[None, :]
    angle = 2.0 * math.pi / SEG * (times * freqs % SEG).astype(jnp.float32)
    return jnp.concatenate([jnp.cos(angle), -jnp.sin(angle)], axis=0).astype(jnp.bfloat16)


def band_rows():
    target = jnp.arange(F, dtype=jnp.int32)[:, None]
    source = jnp.arange(F, dtype=jnp.int32)[None, :]
    inside = jnp.abs(source - target) <= SMOOTH
    counted = (jnp.minimum(target + SMOOTH, F - 1) - jnp.maximum(target - SMOOTH, 0) + 1).astype(
        jnp.float32
    )
    return jnp.where(inside, 1.0 / counted, 0.0)


def lag_table(freq_start, freq_count):
    freqs = (freq_start + jnp.arange(freq_count, dtype=jnp.int32))[:, None]
    shifts = (jnp.arange(LAGS, dtype=jnp.int32) - MAXLAG)[None, :]
    angle = 2.0 * math.pi / SEG * (freqs * shifts % SEG).astype(jnp.float32)
    factor = 1.0 / math.sqrt(F)
    return jnp.concatenate([jnp.cos(angle) * factor, -jnp.sin(angle) * factor], axis=0).astype(
        jnp.bfloat16
    )


def pair_valid(block_idx, stop_idx, num_chan, total_chan, reach):
    rows = jnp.arange(num_chan, dtype=jnp.int32)
    first_chan = block_idx * num_chan + rows
    second_chan = (block_idx + stop_idx) * num_chan + rows
    offset_gap = second_chan[None, :] - first_chan[:, None]
    keep = (offset_gap >= 1) & (offset_gap <= reach[:, None]) & (second_chan[None, :] < total_chan)
    return keep.astype(jnp.float32)


def correlate(own_pair, own_turn, blk_spec, own_mask, blk_mask, lag_tab, valid_pairs):
    freq_rows = blk_spec.shape[0]
    num_chan = blk_spec.shape[3]
    blk_pair = blk_spec.reshape(freq_rows, -1, num_chan)
    cross_re = jnp.einsum("fki,fkj->fij", own_pair, blk_pair, preferred_element_type=jnp.float32)
    cross_im = jnp.einsum("fki,fkj->fij", own_turn, blk_pair, preferred_element_type=jnp.float32)
    counts = jnp.dot(own_mask.T, blk_mask, preferred_element_type=jnp.float32)
    divisor = jnp.maximum(counts, 1.0)[None, :, :]
    stacked = jnp.concatenate([cross_re / divisor, cross_im / divisor], axis=0).astype(jnp.bfloat16)
    lagged = lax.dot_general(
        stacked.reshape(2 * freq_rows, num_chan * num_chan),
        lag_tab,
        (((0,), (0,)), ((), ())),
        preferred_element_type=jnp.float32,
    )
    return lagged.reshape(num_chan, num_chan, -1) * valid_pairs[:, :, None]


def shards(raw_strain, seg_starts, quality_mask, pair_reach):
    num_chan = raw_strain.shape[0]
    seg_local = seg_starts.shape[0]
    section_idx = lax.axis_index("section")
    chan_idx = lax.axis_index("chan")
    section_count = lax.axis_size("section")
    cycle_size = lax.axis_size("chan")
    total_chan = num_chan * cycle_size
    tile_width = num_chan * LAGS
    windows = jax.vmap(
        lambda offset: lax.dynamic_slice_in_dim(raw_strain, offset, SEG, 1), out_axes=0
    )(seg_starts)
    centred = windows - jnp.mean(windows, axis=2, keepdims=True)
    tapered = (centred * hann_window()).astype(jnp.bfloat16)
    spectrum = lax.dot_general(
        dft_rows(),
        tapered.reshape(seg_local * num_chan, SEG),
        (((1,), (1,)), ((), ())),
        preferred_element_type=jnp.float32,
    )
    real_part = spectrum[:F]
    imag_part = spectrum[F:]
    smooth = jnp.dot(
        band_rows(), real_part * real_part + imag_part * imag_part, precision=lax.Precision.HIGHEST
    )
    scale_den = jnp.sqrt(smooth + 1e-06)
    own_rows = lax.dynamic_slice_in_dim(quality_mask, section_idx * seg_local, seg_local, 0).astype(
        jnp.float32
    )
    row_mask = own_rows.reshape(1, seg_local * num_chan)
    real_w = real_part / scale_den * row_mask
    imag_w = imag_part / scale_den * row_mask
    whitened = (
        jnp.stack([real_w, imag_w], axis=1).astype(jnp.bfloat16).reshape(F, 2, seg_local, num_chan)
    )
    mask_wire = quality_mask.astype(jnp.bfloat16)
    own_spec = lax.all_to_all(whitened, "section", split_axis=0, concat_axis=2, tiled=True)
    freq_count = F // section_count
    freq_start = section_idx * freq_count
    local_stops = STOPS
    stop_start = 0
    lag_tab = lag_table(freq_start, freq_count)
    own_pair = own_spec.reshape(freq_count, -1, num_chan)
    own_turn = jnp.concatenate([own_spec[:, 1], -own_spec[:, 0]], axis=1)

    def one_stop(step_idx, block_spec, block_mask):
        valid_pairs = pair_valid(chan_idx, stop_start + step_idx, num_chan, total_chan, pair_reach)
        return correlate(
            own_pair, own_turn, block_spec, mask_wire, block_mask, lag_tab, valid_pairs
        )

    def place_lag(buffer, step_idx, lagged):
        flat_tile = lagged.reshape(num_chan, tile_width)
        return lax.dynamic_update_slice(buffer, flat_tile, (0, step_idx * tile_width))

    lag_buffer = jnp.zeros((num_chan, local_stops * tile_width), jnp.float32)
    lag_buffer = place_lag(lag_buffer, 0, one_stop(0, own_spec, mask_wire))

    def advance(step_idx, state_in):
        buffer, block_spec, block_mask = state_in
        block_spec, block_mask = from_behind((block_spec, block_mask), "chan", -1)
        return (
            place_lag(buffer, step_idx, one_stop(step_idx, block_spec, block_mask)),
            block_spec,
            block_mask,
        )

    lag_buffer = lax.fori_loop(1, local_stops, advance, (lag_buffer, own_spec, mask_wire))[0]
    return lax.psum_scatter(lag_buffer, "section", scatter_dimension=1, tiled=True).astype(
        jnp.bfloat16
    )


def solution(mesh):
    placed = (P("chan", "section"), P("section"), P(None, "chan"), P("chan"))
    return jax.shard_map(
        shards, mesh=mesh, in_specs=placed, out_specs=P("chan", "section"), check_vma=False
    )
```

profile of v0, /device:TPU:0, one launch (start us, length us, event | category | flops | bytes accessed | tf_op | source)
XLA Modules:
  0.0 1296.4 jit_solution(10036192664891877575)
XLA Ops:
  6.6 34.7 %negate_convert_fusion = (bf16[1024,2048]{1,0:T(8,128)(2,1)}, bf16[1024,2048]{1,0:T(8,128)(2,1)}) fusion(), kind=kLoop, calls=%fused_computation.29 | loop fusion | flops 35651584 | bytes 8388608 | tf_op jit(solution)/shard_map/convert.15
  41.5 25.6 %while.20 = (s32[]{:T(128)}, f32[64,10240]{1,0:T(8,128)}, s32[8,2]{0,1:T(2,128)S(1)}, f32[8,64,2048]{2,1,0:T(8,128)}, s32[]{:T(128)}) while((s32[]{:T(128)}, f32[64,10240]{1,0:T(8,128)}, s32[8,2]{0,1:T(2,128)S(1)}, f32[8,64,2048]{2,1,0:T(8,128)}, s32[]{:T(128)}) %tuple.50), condition=%wide.while_cond, body=%wide.while_body.sunk | while | flops 2 | bytes 1049189 | solution.py:91
  111.6 22.7 %all-to-all-done = bf16[2,2,262144]{2,1,0:T(2,128)(2,1)S(1)} async-done(((bf16[2,2,262144]{2,1,0:T(2,128)(2,1)}), bf16[2,2,262144]{2,1,0:T(2,128)(2,1)S(1)}, u32[]{:S(2)}, u32[]{:S(2)}) %all-to-all-start) | async-done | bytes 2097184 | tf_op jit(solution)/shard_map/all_to_all | solution.py:117
  183.3 23.7 %copy.23 = bf16[512,64,64]{0,2,1:T(8,128)(2,1)} copy(bf16[512,64,64]{2,1,0:T(8,128)(2,1)} %divide_convert_fusion.3) | data formatting | bytes 8388608 | tf_op jit(solution)/shard_map/convert.9
  226.6 10.8 dynamic_update_slice.11
  237.4 725.4 %while.19 = (s32[]{:T(128)}, f32[64,102912]{1,0:T(8,128)}, bf16[512,2,16,64]{0,3,2,1:T(8,128)(2,1)}, bf16[16,64]{1,0:T(8,128)(2,1)S(1)}, bf16[512,32,64]{2,1,0:T...) while((s32[]{:T(128)}, f32[64,102912]{1,0:T(8,128)}, ...), condition=%wide.region_2.3_spmd, body=%wide.region_1.2_spmd.sunk | while | flops 1980694784 | bytes 102510320 | solution.py:148
  260.0 9.8 copy.35
  279.2 9.7 copy.34
  308.6 11.5 dynamic_update_slice.13
  326.0 24.5 %collective-permute-done = bf16[16,64]{1,0:T(8,128)(2,1)S(1)} collective-permute-done((bf16[16,64]{1,0:T(8,128)(2,1)S(1)}, bf16[16,64]{1,0:T(8,128)(2,1)S(1)}, u32[]{:S(2)}, u32[]{:S(2)}) %collective-permute-start) | collective-permute-done | bytes 2080 | tf_op jit(solution)/shard_map/while/body/eval_jaxpr/ppermute | solution.py:19
  366.8 9.8 copy.35
  415.5 10.5 dynamic_update_slice.13
  431.8 24.9 %collective-permute-done = bf16[16,64]{1,0:T(8,128)(2,1)S(1)} collective-permute-done((bf16[16,64]{1,0:T(8,128)(2,1)S(1)}, bf16[16,64]{1,0:T(8,128)(2,1)S(1)}, u32[]{:S(2)}, u32[]{:S(2)}) %collective-permute-start) | collective-permute-done | bytes 2080 | tf_op jit(solution)/shard_map/while/body/eval_jaxpr/ppermute | solution.py:19
  472.9 9.8 copy.35
  492.2 9.7 copy.34
  521.6 11.5 dynamic_update_slice.13
  538.9 24.9 %collective-permute-done = bf16[16,64]{1,0:T(8,128)(2,1)S(1)} collective-permute-done((bf16[16,64]{1,0:T(8,128)(2,1)S(1)}, bf16[16,64]{1,0:T(8,128)(2,1)S(1)}, u32[]{:S(2)}, u32[]{:S(2)}) %collective-permute-start) | collective-permute-done | bytes 2080 | tf_op jit(solution)/shard_map/while/body/eval_jaxpr/ppermute | solution.py:19
  580.1 9.8 copy.35
  599.3 9.7 copy.34
  628.7 10.5 dynamic_update_slice.13
  645.1 24.9 %collective-permute-done = bf16[16,64]{1,0:T(8,128)(2,1)S(1)} collective-permute-done((bf16[16,64]{1,0:T(8,128)(2,1)S(1)}, bf16[16,64]{1,0:T(8,128)(2,1)S(1)}, u32[]{:S(2)}, u32[]{:S(2)}) %collective-permute-start) | collective-permute-done | bytes 2080 | tf_op jit(solution)/shard_map/while/body/eval_jaxpr/ppermute | solution.py:19
  686.3 9.8 copy.35
  705.5 9.7 copy.34
  734.9 11.5 dynamic_update_slice.13
  752.3 24.9 %collective-permute-done = bf16[16,64]{1,0:T(8,128)(2,1)S(1)} collective-permute-done((bf16[16,64]{1,0:T(8,128)(2,1)S(1)}, bf16[16,64]{1,0:T(8,128)(2,1)S(1)}, u32[]{:S(2)}, u32[]{:S(2)}) %collective-permute-start) | collective-permute-done | bytes 2080 | tf_op jit(solution)/shard_map/while/body/eval_jaxpr/ppermute | solution.py:19
  793.5 9.8 copy.35
  812.7 9.7 copy.34
  842.1 10.5 dynamic_update_slice.13
  858.5 24.9 %collective-permute-done = bf16[16,64]{1,0:T(8,128)(2,1)S(1)} collective-permute-done((bf16[16,64]{1,0:T(8,128)(2,1)S(1)}, bf16[16,64]{1,0:T(8,128)(2,1)S(1)}, u32[]{:S(2)}, u32[]{:S(2)}) %collective-permute-start) | collective-permute-done | bytes 2080 | tf_op jit(solution)/shard_map/while/body/eval_jaxpr/ppermute | solution.py:19
  899.6 9.8 copy.35
  948.3 11.4 dynamic_update_slice.13
  962.8 318.4 %reduce-scatter.2.cloned.1.call-done = f32[64,51456]{1,0:T(8,128)} async-done(((f32[64,102912]{1,0:T(8,128)}), f32[64,51456]{1,0:T(8,128)}) %reduce-scatter.2.cloned.1.call-update) | async-done | bytes 13172752 | tf_op jit(solution)/shard_map/reduce_scatter | solution.py:149
  (220 shorter events, 528.6 us)
Async XLA Ops:
  6.6 34.7 %copy-start.6 = (s32[8]{0:T(128)S(1)}, s32[8]{0:T(128)}, u32[]{:S(2)}) copy-start(s32[8]{0:T(128)} %param.7) | copy-start | bytes 100
  6.6 34.7 %copy-start.5 = (s32[16,64]{1,0:T(8,128)S(1)}, s32[16,64]{1,0:T(8,128)}, u32[]{:S(2)}) copy-start(s32[16,64]{1,0:T(8,128)} %param.8) | copy-start | bytes 12292
  104.1 30.2 %all-to-all-start = ((bf16[2,2,262144]{2,1,0:T(2,128)(2,1)}), bf16[2,2,262144]{2,1,0:T(2,128)(2,1)S(1)}, u32[]{:S(2)}, u32[]{:S(2)}) async-start(bf16[2,2,262144]{2,1,0:T(2,128)(2,1)} %reshape.285), calls=%async_computation | async-start | bytes 4194304 | tf_op jit(solution)/shard_map/all_to_all | solution.py:117
  108.5 1172.7 %reduce-scatter.2.cloned.1.call-start = ((), (), s32[]{:S(2)}) async-start(), calls=%async_computation.2 | async-start | bytes 39518208 | tf_op jit(solution)/shard_map/reduce_scatter | solution.py:149
  237.4 6.4 collective-permute-start.1
  238.7 5.0 collective-permute-start
  243.8 16.1 %copy-start = (bf16[512,2,16,64]{0,3,2,1:T(8,128)(2,1)}, bf16[512,2,16,64]{0,3,2,1:T(8,128)(2,1)S(1)}, u32[]{:S(2)}) copy-start(bf16[512,2,16,64]{0,3,2,1:T(8,128)(2,1)S(1)} %collective-permute-done.1) | copy-start | bytes 6291460 | tf_op jit(solution)/shard_map/while
  288.9 8.0 copy-start.3
  323.2 27.4 %collective-permute-start.1 = (bf16[512,2,16,64]{0,3,2,1:T(8,128)(2,1)}, bf16[512,2,16,64]{0,3,2,1:T(8,128)(2,1)S(1)}, u32[]{:S(2)}, u32[]{:S(2)}) collective-permute-start(bf16[512,2,16,64]{0,3,2,1:T(8,128)(2,1)} %get-tuple-element.424), channel_id=1, source_target_pairs={{1,0},{2,1},{3,2},{4,3},{5,4},{6,5},{7,6},{8,7},{9,8},{10,9},{11,1... | collective-permute-start | bytes 6291464 | tf_op jit(solution)/shard_map/while/body/eval_jaxpr/ppermute | solution.py:19
  324.5 26.0 %collective-permute-start = (bf16[16,64]{1,0:T(8,128)(2,1)S(1)}, bf16[16,64]{1,0:T(8,128)(2,1)S(1)}, u32[]{:S(2)}, u32[]{:S(2)}) collective-permute-start(bf16[16,64]{1,0:T(8,128)(2,1)S(1)} %get-tuple-element.425), channel_id=1, source_target_pairs={{1,0},{2,1},{3,2},{4,3},{5,4},{6,5},{7,6},{8,7},{9,8},{10,9},{11,1... | collective-permute-start | bytes 6152 | tf_op jit(solution)/shard_map/while/body/eval_jaxpr/ppermute | solution.py:19
  350.7 16.1 %copy-start = (bf16[512,2,16,64]{0,3,2,1:T(8,128)(2,1)}, bf16[512,2,16,64]{0,3,2,1:T(8,128)(2,1)S(1)}, u32[]{:S(2)}) copy-start(bf16[512,2,16,64]{0,3,2,1:T(8,128)(2,1)S(1)} %collective-permute-done.1) | copy-start | bytes 6291460 | tf_op jit(solution)/shard_map/while
  395.8 8.0 copy-start.3
  429.0 27.8 %collective-permute-start.1 = (bf16[512,2,16,64]{0,3,2,1:T(8,128)(2,1)}, bf16[512,2,16,64]{0,3,2,1:T(8,128)(2,1)S(1)}, u32[]{:S(2)}, u32[]{:S(2)}) collective-permute-start(bf16[512,2,16,64]{0,3,2,1:T(8,128)(2,1)} %get-tuple-element.424), channel_id=1, source_target_pairs={{1,0},{2,1},{3,2},{4,3},{5,4},{6,5},{7,6},{8,7},{9,8},{10,9},{11,1... | collective-permute-start | bytes 6291464 | tf_op jit(solution)/shard_map/while/body/eval_jaxpr/ppermute | solution.py:19
  430.3 26.3 %collective-permute-start = (bf16[16,64]{1,0:T(8,128)(2,1)S(1)}, bf16[16,64]{1,0:T(8,128)(2,1)S(1)}, u32[]{:S(2)}, u32[]{:S(2)}) collective-permute-start(bf16[16,64]{1,0:T(8,128)(2,1)S(1)} %get-tuple-element.425), channel_id=1, source_target_pairs={{1,0},{2,1},{3,2},{4,3},{5,4},{6,5},{7,6},{8,7},{9,8},{10,9},{11,1... | collective-permute-start | bytes 6152 | tf_op jit(solution)/shard_map/while/body/eval_jaxpr/ppermute | solution.py:19
  456.8 16.1 %copy-start = (bf16[512,2,16,64]{0,3,2,1:T(8,128)(2,1)}, bf16[512,2,16,64]{0,3,2,1:T(8,128)(2,1)S(1)}, u32[]{:S(2)}) copy-start(bf16[512,2,16,64]{0,3,2,1:T(8,128)(2,1)S(1)} %collective-permute-done.1) | copy-start | bytes 6291460 | tf_op jit(solution)/shard_map/while
  501.9 8.0 copy-start.3
  536.2 27.8 %collective-permute-start.1 = (bf16[512,2,16,64]{0,3,2,1:T(8,128)(2,1)}, bf16[512,2,16,64]{0,3,2,1:T(8,128)(2,1)S(1)}, u32[]{:S(2)}, u32[]{:S(2)}) collective-permute-start(bf16[512,2,16,64]{0,3,2,1:T(8,128)(2,1)} %get-tuple-element.424), channel_id=1, source_target_pairs={{1,0},{2,1},{3,2},{4,3},{5,4},{6,5},{7,6},{8,7},{9,8},{10,9},{11,1... | collective-permute-start | bytes 6291464 | tf_op jit(solution)/shard_map/while/body/eval_jaxpr/ppermute | solution.py:19
  537.5 26.3 %collective-permute-start = (bf16[16,64]{1,0:T(8,128)(2,1)S(1)}, bf16[16,64]{1,0:T(8,128)(2,1)S(1)}, u32[]{:S(2)}, u32[]{:S(2)}) collective-permute-start(bf16[16,64]{1,0:T(8,128)(2,1)S(1)} %get-tuple-element.425), channel_id=1, source_target_pairs={{1,0},{2,1},{3,2},{4,3},{5,4},{6,5},{7,6},{8,7},{9,8},{10,9},{11,1... | collective-permute-start | bytes 6152 | tf_op jit(solution)/shard_map/while/body/eval_jaxpr/ppermute | solution.py:19
  563.9 16.1 %copy-start = (bf16[512,2,16,64]{0,3,2,1:T(8,128)(2,1)}, bf16[512,2,16,64]{0,3,2,1:T(8,128)(2,1)S(1)}, u32[]{:S(2)}) copy-start(bf16[512,2,16,64]{0,3,2,1:T(8,128)(2,1)S(1)} %collective-permute-done.1) | copy-start | bytes 6291460 | tf_op jit(solution)/shard_map/while
  609.0 8.0 copy-start.3
  642.4 27.8 %collective-permute-start.1 = (bf16[512,2,16,64]{0,3,2,1:T(8,128)(2,1)}, bf16[512,2,16,64]{0,3,2,1:T(8,128)(2,1)S(1)}, u32[]{:S(2)}, u32[]{:S(2)}) collective-permute-start(bf16[512,2,16,64]{0,3,2,1:T(8,128)(2,1)} %get-tuple-element.424), channel_id=1, source_target_pairs={{1,0},{2,1},{3,2},{4,3},{5,4},{6,5},{7,6},{8,7},{9,8},{10,9},{11,1... | collective-permute-start | bytes 6291464 | tf_op jit(solution)/shard_map/while/body/eval_jaxpr/ppermute | solution.py:19
  643.7 26.3 %collective-permute-start = (bf16[16,64]{1,0:T(8,128)(2,1)S(1)}, bf16[16,64]{1,0:T(8,128)(2,1)S(1)}, u32[]{:S(2)}, u32[]{:S(2)}) collective-permute-start(bf16[16,64]{1,0:T(8,128)(2,1)S(1)} %get-tuple-element.425), channel_id=1, source_target_pairs={{1,0},{2,1},{3,2},{4,3},{5,4},{6,5},{7,6},{8,7},{9,8},{10,9},{11,1... | collective-permute-start | bytes 6152 | tf_op jit(solution)/shard_map/while/body/eval_jaxpr/ppermute | solution.py:19
  670.2 16.1 %copy-start = (bf16[512,2,16,64]{0,3,2,1:T(8,128)(2,1)}, bf16[512,2,16,64]{0,3,2,1:T(8,128)(2,1)S(1)}, u32[]{:S(2)}) copy-start(bf16[512,2,16,64]{0,3,2,1:T(8,128)(2,1)S(1)} %collective-permute-done.1) | copy-start | bytes 6291460 | tf_op jit(solution)/shard_map/while
  715.2 8.0 copy-start.3
  749.5 27.8 %collective-permute-start.1 = (bf16[512,2,16,64]{0,3,2,1:T(8,128)(2,1)}, bf16[512,2,16,64]{0,3,2,1:T(8,128)(2,1)S(1)}, u32[]{:S(2)}, u32[]{:S(2)}) collective-permute-start(bf16[512,2,16,64]{0,3,2,1:T(8,128)(2,1)} %get-tuple-element.424), channel_id=1, source_target_pairs={{1,0},{2,1},{3,2},{4,3},{5,4},{6,5},{7,6},{8,7},{9,8},{10,9},{11,1... | collective-permute-start | bytes 6291464 | tf_op jit(solution)/shard_map/while/body/eval_jaxpr/ppermute | solution.py:19
  750.8 26.3 %collective-permute-start = (bf16[16,64]{1,0:T(8,128)(2,1)S(1)}, bf16[16,64]{1,0:T(8,128)(2,1)S(1)}, u32[]{:S(2)}, u32[]{:S(2)}) collective-permute-start(bf16[16,64]{1,0:T(8,128)(2,1)S(1)} %get-tuple-element.425), channel_id=1, source_target_pairs={{1,0},{2,1},{3,2},{4,3},{5,4},{6,5},{7,6},{8,7},{9,8},{10,9},{11,1... | collective-permute-start | bytes 6152 | tf_op jit(solution)/shard_map/while/body/eval_jaxpr/ppermute | solution.py:19
  777.3 16.1 %copy-start = (bf16[512,2,16,64]{0,3,2,1:T(8,128)(2,1)}, bf16[512,2,16,64]{0,3,2,1:T(8,128)(2,1)S(1)}, u32[]{:S(2)}) copy-start(bf16[512,2,16,64]{0,3,2,1:T(8,128)(2,1)S(1)} %collective-permute-done.1) | copy-start | bytes 6291460 | tf_op jit(solution)/shard_map/while
  822.4 8.0 copy-start.3
  855.7 27.8 %collective-permute-start.1 = (bf16[512,2,16,64]{0,3,2,1:T(8,128)(2,1)}, bf16[512,2,16,64]{0,3,2,1:T(8,128)(2,1)S(1)}, u32[]{:S(2)}, u32[]{:S(2)}) collective-permute-start(bf16[512,2,16,64]{0,3,2,1:T(8,128)(2,1)} %get-tuple-element.424), channel_id=1, source_target_pairs={{1,0},{2,1},{3,2},{4,3},{5,4},{6,5},{7,6},{8,7},{9,8},{10,9},{11,1... | collective-permute-start | bytes 6291464 | tf_op jit(solution)/shard_map/while/body/eval_jaxpr/ppermute | solution.py:19
  857.0 26.3 %collective-permute-start = (bf16[16,64]{1,0:T(8,128)(2,1)S(1)}, bf16[16,64]{1,0:T(8,128)(2,1)S(1)}, u32[]{:S(2)}, u32[]{:S(2)}) collective-permute-start(bf16[16,64]{1,0:T(8,128)(2,1)S(1)} %get-tuple-element.425), channel_id=1, source_target_pairs={{1,0},{2,1},{3,2},{4,3},{5,4},{6,5},{7,6},{8,7},{9,8},{10,9},{11,1... | collective-permute-start | bytes 6152 | tf_op jit(solution)/shard_map/while/body/eval_jaxpr/ppermute | solution.py:19
  883.5 16.1 %copy-start = (bf16[512,2,16,64]{0,3,2,1:T(8,128)(2,1)}, bf16[512,2,16,64]{0,3,2,1:T(8,128)(2,1)S(1)}, u32[]{:S(2)}) copy-start(bf16[512,2,16,64]{0,3,2,1:T(8,128)(2,1)S(1)} %collective-permute-done.1) | copy-start | bytes 6291460 | tf_op jit(solution)/shard_map/while
  928.6 8.0 copy-start.3
  (3 other events, 14.1 us)
Sparse Core Ops, SparseCore 0:
  962.9 318.2 reduce-scatter.1
where the time goes:
time: 1310 us; the launch traced here: 1300 us
  waiting for transfers between devices  493 us (38%)
  local copies, waits for them, and re-layouts  414 us (32%)
  matrix products  227 us (17%)
  other arithmetic  126 us (10%)
  starting transfers between devices  22.4 us (2%)
  between operations  13.8 us (1%)
    reduce_scatter x1, waiting for transfers between devices, shards(): lax.psum_scatter(lag_buffer, 'section', scatter_dimension=1, tiled=True)  318 us
    another operation x16, local copies, waits for them, and re-layouts  170 us
    ppermute x14, waiting for transfers between devices, from_behind(): return lax.ppermute(block, axis, route)  152 us
    dynamic_update_slice x8, local copies, waits for them, and re-layouts, place_lag(): lax.dynamic_update_slice(buffer, flat_tile, (0, step_idx * tile_width))  88.2 us
    dot_general x8, matrix products, correlate(): jnp.einsum('fki,fkj->fij', own_pair, blk_pair, preferred_element_type=jnp...  75.6 us
    dot_general x8, matrix products, correlate(): jnp.einsum('fki,fkj->fij', own_turn, blk_pair, preferred_element_type=jnp...  72.9 us
    concatenate x8, other arithmetic, correlate(): jnp.concatenate([cross_re / divisor, cross_im / divisor], axis=0)  63.6 us
    dot_general x8, matrix products, correlate(): lax.dot_general(stacked.reshape(2 * freq_rows, num_chan * num_chan), lag_...  61.7 us
  transfers between devices with their start and end apart: 16, of which 9 were waited for; matrix products, arithmetic and copies ran while one was open for 0% of the time, Pallas kernels for 0%

commit v1 on v0

v1 whole, which is shorter than its diff:
```python
import math

import jax
import jax.numpy as jnp
from jax import lax
from jax.experimental import pallas as pl
from jax.experimental.pallas import tpu as pltpu
from jax.sharding import PartitionSpec as P

SEG = 2048
F = 1024
SMOOTH = 64
MAXLAG = 100
LAGS = 201
STOPS = 8


def hann_window():
    steps = jnp.arange(SEG, dtype=jnp.int32).astype(jnp.float32)
    return 0.5 - 0.5 * jnp.cos(2.0 * math.pi / SEG * steps)


def dft_rows():
    freqs = jnp.arange(F, dtype=jnp.int32)[:, None]
    times = jnp.arange(SEG, dtype=jnp.int32)[None, :]
    angle = 2.0 * math.pi / SEG * (times * freqs % SEG).astype(jnp.float32)
    return jnp.concatenate([jnp.cos(angle), -jnp.sin(angle)], axis=0).astype(jnp.bfloat16)


def band_rows():
    target = jnp.arange(F, dtype=jnp.int32)[:, None]
    source = jnp.arange(F, dtype=jnp.int32)[None, :]
    inside = jnp.abs(source - target) <= SMOOTH
    counted = (jnp.minimum(target + SMOOTH, F - 1) - jnp.maximum(target - SMOOTH, 0) + 1).astype(
        jnp.float32
    )
    return jnp.where(inside, 1.0 / counted, 0.0)


GROUP = 8
LAG_ROWS = 208
ROWS = 32
STEPS = 8


def lag_rows():
    freqs = jnp.arange(F, dtype=jnp.int32)[None, :]
    shifts = (jnp.arange(LAG_ROWS, dtype=jnp.int32) - MAXLAG)[:, None]
    angle = 2.0 * math.pi / SEG * (freqs * shifts % SEG).astype(jnp.float32)
    factor = 1.0 / math.sqrt(F)
    both = jnp.stack([jnp.cos(angle) * factor, -jnp.sin(angle) * factor], axis=1)
    both = jnp.where(shifts[:, :, None] <= MAXLAG, both, 0.0)
    both = both.reshape(LAG_ROWS, 2, F // GROUP, GROUP).transpose(0, 2, 1, 3)
    return both.reshape(LAG_ROWS, 2 * F).astype(jnp.bfloat16)


def correlate_kernel(*refs):
    pair_ref, turn_ref = refs[0], refs[1]
    blocks = refs[2:10]
    lag_ref, scale_ref, out_ref, cross, lagged = refs[10:]
    step = pl.program_id(1)
    rows = pair_ref.shape[2]
    depth = pair_ref.shape[3]
    groups = pair_ref.shape[1]
    half_depth = depth // 2
    per_freq = half_depth // GROUP
    chans = blocks[0].shape[1] // 2
    cols = 4 * chans
    lane = lax.broadcasted_iota(jnp.int32, (GROUP, depth), 1)
    row = lax.broadcasted_iota(jnp.int32, (GROUP, depth), 0)
    keep = (lax.rem(lane, half_depth) // per_freq == row)[None]

    def one_group(g, carry):
        at = pl.multiple_of(g * half_depth, half_depth)
        tiles = [ref[pl.ds(at, half_depth), :] for ref in blocks]
        for fh in range(2):
            cut = slice(fh * chans, (fh + 1) * chans)
            mine = jnp.concatenate([t[:, cut] for t in tiles[:4]], axis=1)
            other = jnp.concatenate([t[:, cut] for t in tiles[4:]], axis=1)
            weights = jnp.concatenate([mine, other], axis=0)
            pair = pair_ref[fh, g].astype(jnp.float32)[:, None, :]
            turn = turn_ref[fh, g].astype(jnp.float32)[:, None, :]
            spread = jnp.concatenate(
                [jnp.where(keep, pair, 0.0), jnp.where(keep, turn, 0.0)], axis=1
            )
            spread = spread.reshape(rows * 2 * GROUP, depth).astype(jnp.bfloat16)
            product = jnp.dot(spread, weights, preferred_element_type=jnp.float32)
            place = (fh * groups * pl.num_programs(1) + step * groups + g) * 2 * GROUP
            cross[:, pl.ds(pl.multiple_of(place, 2 * GROUP), 2 * GROUP), :] = product.astype(
                jnp.bfloat16
            ).reshape(rows, 2 * GROUP, cols)
        return carry

    lax.fori_loop(0, groups, one_group, 0)

    @pl.when(step == pl.num_programs(1) - 1)
    def finish():
        def one_row(i, carry):
            value = jnp.dot(lag_ref[...], cross[i], preferred_element_type=jnp.float32)
            value = value * scale_ref[pl.ds(i, 1), :]
            value = jnp.concatenate(
                [value, jnp.zeros((256 - LAG_ROWS, cols), jnp.float32)], axis=0
            )
            lagged[:, pl.ds(i, 1), :] = value.T[:, None, :]
            return carry

        lax.fori_loop(0, rows, one_row, 0)
        lanes = lax.broadcasted_iota(jnp.int32, (rows, 128), 1)

        def span(h, carry):
            base = h * 128
            out_at = h * (128 * LAGS)
            waiting = {}
            for j in range(128):
                tile, shift = divmod(j * LAGS, 128)
                block = lagged[base + j]
                if shift:
                    block = pltpu.roll(block, shift, 1)
                first, second = block[:, :128], block[:, 128:]
                if shift:
                    parts = (
                        jnp.where(lanes >= shift, first, 0.0),
                        second,
                        jnp.where(lanes < shift, first, 0.0),
                    )
                else:
                    parts = (first, second)
                for t, part in enumerate(parts):
                    have = waiting.get(tile + t)
                    waiting[tile + t] = part if have is None else have + part
                upto = (j + 1) * LAGS // 128
                for t in sorted(waiting):
                    if t < upto:
                        done = waiting.pop(t)
                        out_ref[:, pl.ds(pl.multiple_of(out_at + t * 128, 128), 128)] = (
                            done.astype(out_ref.dtype)
                        )
            return carry

        lax.fori_loop(0, cols // 128, span, 0)


def correlate(pair, turn, blocks, lags, scale):
    num_chan = pair.shape[2]
    rows = min(ROWS, num_chan)
    groups = pair.shape[1] // STEPS
    block_rows = blocks[0].shape[0] // STEPS
    cols = scale.shape[1]
    own_spec = pl.BlockSpec((2, groups, rows, pair.shape[3]), lambda i, g: (0, g, i, 0))
    blk_spec = pl.BlockSpec((block_rows, 2 * num_chan), lambda i, g: (g, 0))
    return pl.pallas_call(
        correlate_kernel,
        grid=(num_chan // rows, STEPS),
        out_shape=jax.ShapeDtypeStruct((num_chan, cols * LAGS), jnp.bfloat16),
        in_specs=[own_spec, own_spec]
        + [blk_spec] * 8
        + [
            pl.BlockSpec((LAG_ROWS, 2 * F), lambda i, g: (0, 0)),
            pl.BlockSpec((rows, cols), lambda i, g: (i, 0)),
        ],
        out_specs=pl.BlockSpec((rows, cols * LAGS), lambda i, g: (i, 0)),
        scratch_shapes=[
            pltpu.VMEM((rows, 2 * F, cols), jnp.bfloat16),
            pltpu.VMEM((cols, rows, 256), jnp.float32),
        ],
        compiler_params=pltpu.CompilerParams(vmem_limit_bytes=67043328 - 1024 * 1024),
    )(pair, turn, *blocks, lags, scale)


def swap_section(value):
    count = lax.axis_size("section")
    return lax.ppermute(value, "section", [(i, count - 1 - i) for i in range(count)])


def fetch(value, route):
    return lax.ppermute(value, "chan", route)


def shards(raw_strain, seg_starts, quality_mask, pair_reach):
    num_chan = raw_strain.shape[0]
    seg_local = seg_starts.shape[0]
    section_idx = lax.axis_index("section")
    chan_idx = lax.axis_index("chan")
    cycle_size = lax.axis_size("chan")
    total_chan = num_chan * cycle_size
    windows = jax.vmap(
        lambda offset: lax.dynamic_slice_in_dim(raw_strain, offset, SEG, 1), out_axes=0
    )(seg_starts)
    centred = windows - jnp.mean(windows, axis=2, keepdims=True)
    tapered = (centred * hann_window()).astype(jnp.bfloat16)
    spectrum = lax.dot_general(
        dft_rows(),
        tapered.reshape(seg_local * num_chan, SEG),
        (((1,), (1,)), ((), ())),
        preferred_element_type=jnp.float32,
    )
    real_part = spectrum[:F]
    imag_part = spectrum[F:]
    smooth = jnp.dot(
        band_rows(), real_part * real_part + imag_part * imag_part, precision=lax.Precision.HIGHEST
    )
    own_rows = lax.dynamic_slice_in_dim(quality_mask, section_idx * seg_local, seg_local, 0).astype(
        jnp.float32
    )
    gain = own_rows.reshape(1, seg_local * num_chan) / jnp.sqrt(smooth + 1e-06)
    white = jnp.stack([real_part * gain, imag_part * gain], axis=1).astype(jnp.bfloat16)
    own = (
        white.reshape(2, F // 2, 2 * seg_local, num_chan)
        .transpose(1, 2, 0, 3)
        .reshape(F * seg_local, 2 * num_chan)
    )

    first = section_idx == 0
    odd_pair = (chan_idx // 2) % 2 == 1
    odd = chan_idx % 2 == 1
    chans = range(cycle_size)
    up4 = [(i, i - 4) for i in chans if i >= 4]
    pair_swap = [(i, i ^ 2) for i in chans]
    core_swap = [(i, i ^ 1) for i in chans]
    own_far = swap_section(own)
    plus4 = fetch(own, up4)
    plus8 = fetch(plus4, up4)
    plus2 = fetch(jnp.where(odd_pair, own, plus4), pair_swap)
    plus6 = fetch(jnp.where(odd_pair, plus4, plus8), pair_swap)
    a0 = jnp.where(first, own, plus4)
    a0_far = swap_section(jnp.where(first, plus4, own))
    a2 = jnp.where(first, plus2, plus6)
    a2_far = swap_section(jnp.where(first, plus6, plus2))
    a4 = jnp.where(first, plus4, plus8)
    a4_far = swap_section(jnp.where(first, plus8, plus4))
    b1 = fetch(jnp.where(odd, a0, a2), core_swap)
    b1_far = fetch(jnp.where(odd, a0_far, a2_far), core_swap)
    b3 = fetch(jnp.where(odd, a2, a4), core_swap)
    b3_far = fetch(jnp.where(odd, a2_far, a4_far), core_swap)

    halves = jnp.stack([own, own_far]).reshape(
        2, F // 2 // GROUP, GROUP, 2, seg_local, 2, num_chan
    )
    turned = jnp.stack([halves[:, :, :, 1], -halves[:, :, :, 0]], axis=3)

    def own_side(value):
        return value.transpose(5, 1, 6, 0, 2, 3, 4).reshape(
            2, F // 2 // GROUP, num_chan, 4 * GROUP * seg_local
        )

    stops_here = STOPS // lax.axis_size("section")
    stop_start = section_idx * stops_here
    wide = lax.all_gather(quality_mask, "chan", axis=1, tiled=True)
    wide = jnp.pad(wide, ((0, 0), (0, STOPS * num_chan))).astype(jnp.float32)
    first_col = (chan_idx + stop_start) * num_chan
    other_mask = lax.dynamic_slice_in_dim(wide, first_col, stops_here * num_chan, 1)
    counts = jnp.dot(
        quality_mask.astype(jnp.float32).T, other_mask, preferred_element_type=jnp.float32
    )
    first_chan = chan_idx * num_chan + jnp.arange(num_chan, dtype=jnp.int32)
    second_chan = first_col + jnp.arange(stops_here * num_chan, dtype=jnp.int32)
    gap = second_chan[None, :] - first_chan[:, None]
    valid = (gap >= 1) & (gap <= pair_reach[:, None]) & (second_chan[None, :] < total_chan)
    scale = jnp.where(valid, 1.0 / jnp.maximum(counts, 1.0), 0.0)

    return correlate(
        own_side(halves),
        own_side(turned),
        (a0, b1, a2, b3, a0_far, b1_far, a2_far, b3_far),
        lag_rows(),
        scale,
    )


def solution(mesh):
    placed = (P("chan", "section"), P("section"), P(None, "chan"), P("chan"))
    return jax.shard_map(
        shards, mesh=mesh, in_specs=placed, out_specs=P("chan", "section"), check_vma=False
    )
```

time: 1310 us -> 599 us (0.46)
  local copies, waits for them, and re-layouts: 414 us -> 107 us
  waiting for transfers between devices: 493 us -> 263 us
  matrix products: 227 us -> 14.8 us
  Pallas kernels: 0 us -> 102 us
  other arithmetic: 126 us -> 82.6 us
  blocking collectives: 0 us -> 18.6 us
  between operations: 13.8 us -> 0.24 us
    reduce_scatter x1 -> x0, waiting for transfers between devices: 318 us -> none  [shards(): lax.psum_scatter(lag_buffer, 'section', scatter_dimension=1, tiled=True)]
    dot_general x32 -> x1, matrix products: 212 us -> 0.86 us  [shards(): jnp.dot(quality_mask.astype(jnp.float32).T, other_mask, preferred_element...]
    another operation x18 -> x3, local copies, waits for them, and re-layouts: 175 us -> 15.9 us  [the longest x2 13.5 us: shards(): jnp.stack([own, own_far])]
    ppermute x14 -> x12, waiting for transfers between devices: 152 us -> 263 us  [the longest x8 180 us: fetch(): return lax.ppermute(value, 'chan', route)]
    pallas_call x0 -> x1, Pallas kernels: none -> 102 us  [correlate(): pl.pallas_call(correlate_kernel, grid=(num_chan // rows, STEPS), out_shap...]
    dynamic_update_slice x8 -> x0, local copies, waits for them, and re-layouts: 88.2 us -> none  [place_lag(): lax.dynamic_update_slice(buffer, flat_tile, (0, step_idx * tile_width))]
    concatenate x10 -> x0, other arithmetic: 67.3 us -> none  [the longest x8 63.6 us: correlate(): jnp.concatenate([cross_re / divisor, cross_im / divisor], axis=0)]
    ppermute x7 -> x0, local copies, waits for them, and re-layouts: 46.6 us -> none  [from_behind(): return lax.ppermute(block, axis, route)]
  transfers between devices with their start and end apart: 16 -> 12, of which waited for: 9 -> 6; matrix products, arithmetic and copies ran while one was open for 0% -> 16% of each run, Pallas kernels for 0% -> 0%
where the time goes in v1:
time: 599 us; the launch traced here: 598 us
  waiting for transfers between devices  263 us (44%)
  local copies, waits for them, and re-layouts  107 us (18%)
  Pallas kernels  102 us (17%)
  other arithmetic  82.6 us (14%)
  blocking collectives  18.6 us (3%)
  matrix products  14.8 us (2%)
  starting transfers between devices  9.71 us (2%)
    ppermute x8, waiting for transfers between devices, fetch(): return lax.ppermute(value, 'chan', route)  180 us
    pallas_call x1, Pallas kernels, correlate(): pl.pallas_call(correlate_kernel, grid=(num_chan // rows, STEPS), out_shap...  102 us
    ppermute x4, waiting for transfers between devices, swap_section(): lax.ppermute(value, 'section', [(i, count - 1 - i) for i in range(count)])  83.4 us
    another operation x1, other arithmetic  34.7 us
    gather x24, local copies, waits for them, and re-layouts  27.4 us
    all_gather x1, blocking collectives, shards(): wide = lax.all_gather(quality_mask, 'chan', axis=1, tiled=True)  18.6 us
    transpose x2, local copies, waits for them, and re-layouts, own_side(): value.transpose(5, 1, 6, 0, 2, 3, 4)  18.5 us
    reshape x2, local copies, waits for them, and re-layouts, own_side(): value.transpose(5, 1, 6, 0, 2, 3, 4)  17.1 us
  transfers between devices with their start and end apart: 12, of which 6 were waited for; matrix products, arithmetic and copies ran while one was open for 16% of the time, Pallas kernels for 0%

profile of v1, /device:TPU:0, one launch (start us, length us, event | category | flops | bytes accessed | tf_op | source)
XLA Modules:
  0.0 597.9 jit_solution(18153654193950205554)
XLA Ops:
  0.1 34.7 %negate_convert_fusion = (bf16[1024,2048]{1,0:T(8,128)(2,1)}, bf16[1024,2048]{1,0:T(8,128)(2,1)}) fusion(), kind=kLoop, calls=%fused_computation.19 | loop fusion | flops 35651584 | bytes 8388608 | tf_op jit(solution)/shard_map/convert.5
  34.8 27.4 %while.1 = (s32[]{:T(128)}, f32[64,10240]{1,0:T(8,128)}, s32[8,2]{0,1:T(2,128)S(1)}, f32[8,64,2048]{2,1,0:T(8,128)}, s32[]{:T(128)}) while((s32[]{:T(128)}, f32[64,10240]{1,0:T(8,128)}, s32[8,2]{0,1:T(2,128)S(1)}, f32[8,64,2048]{2,1,0:T(8,128)}, s32[]{:T(128)}) %tuple.27), condition=%wide.while_cond, body=%wide.while_body.sunk | while | flops 2 | bytes 1049189 | solution.py:187
  35.5 2.7 bitcast_dynamic-update-slice_fusion.2
  42.4 2.7 bitcast_dynamic-update-slice_fusion.2
  64.8 2.8 fusion.15
  68.3 6.7 %fusion.4 = f32[2048,512]{1,0:T(8,128)S(1)} fusion(bf16[512,2048]{1,0:T(8,128)(2,1)S(1)} %fusion.15, bf16[1024,2048]{1,0:T(8,128)(2,1)S(1)} %copy-done.4, bf16[1024,2048]{1,0:T(8,128)(2,1)} %get-tuple-element.39), kind=kOutput, calls=%fused_computation.14 | convolution fusion | flops 4311744512 | bytes 14680064 | tf_op jit(solution)/shard_map/dot_general | solution.py:191
  75.0 7.2 %fusion.33 = (bf16[1024,1,512]{2,0,1:T(8,128)(2,1)S(1)}, bf16[1024,1,512]{2,0,1:T(8,128)(2,1)S(1)}) fusion(f32[2048,512]{1,0:T(8,128)S(1)} %fusion.4, f32[512]{0:T(512)S(1)} %div.46, f32[1024]{0:T(1024)S(1)} %fusion.44), kind=kOutput, calls=%fused_computation.70 | convolution fusion | flops 6451363840 | bytes 10491904 | tf_op jit(solution)/shard_map/dot_general | solution.py:199
  84.8 3.3 convert_element_type.69
  88.2 8.1 %copy.36 = bf16[512,16,2,64]{3,2,1,0:T(2,128)(2,1)} copy(bf16[512,16,2,64]{0,2,3,1:T(2,128)(2,1)S(1)} %bitcast.47) | data formatting | bytes 4194304 | tf_op jit(solution)/shard_map/transpose | solution.py:209
  96.2 7.8 %reshape.175 = bf16[8192,128]{1,0:T(8,128)(2,1)} reshape(bf16[512,16,2,64]{3,2,1,0:T(2,128)(2,1)} %copy.36) | data formatting | bytes 4194304 | tf_op jit(solution)/shard_map/reshape | solution.py:210
  105.3 49.6 %collective-permute-done.1 = bf16[8192,128]{1,0:T(8,128)(2,1)} collective-permute-done((bf16[8192,128]{1,0:T(8,128)(2,1)}, bf16[8192,128]{1,0:T(8,128)(2,1)}, u32[]{:S(2)}, u32[]{:S(2)}) %collective-permute-start.1) | collective-permute-done | bytes 2097184 | tf_op jit(solution)/shard_map/ppermute | solution.py:176
  156.2 47.7 %collective-permute-done.3 = bf16[8192,128]{1,0:T(8,128)(2,1)} collective-permute-done((bf16[8192,128]{1,0:T(8,128)(2,1)}, bf16[8192,128]{1,0:T(8,128)(2,1)}, u32[]{:S(2)}, u32[]{:S(2)}) %collective-permute-start.3) | collective-permute-done | bytes 2097184 | tf_op jit(solution)/shard_map/ppermute | solution.py:176
  203.9 5.8 broadcast_select_fusion.7
  213.1 4.6 cosine_multiply_fusion
  218.5 40.0 %collective-permute-done.2 = bf16[8192,128]{1,0:T(8,128)(2,1)} collective-permute-done((bf16[8192,128]{1,0:T(8,128)(2,1)}, bf16[8192,128]{1,0:T(8,128)(2,1)}, u32[]{:S(2)}, u32[]{:S(2)}) %collective-permute-start.2) | collective-permute-done | bytes 2097184 | tf_op jit(solution)/shard_map/ppermute | solution.py:176
  258.5 42.4 %collective-permute-done.4 = bf16[8192,128]{1,0:T(8,128)(2,1)} collective-permute-done((bf16[8192,128]{1,0:T(8,128)(2,1)}, bf16[8192,128]{1,0:T(8,128)(2,1)}, u32[]{:S(2)}, u32[]{:S(2)}) %collective-permute-start.4) | collective-permute-done | bytes 2097184 | tf_op jit(solution)/shard_map/ppermute | solution.py:176
  300.9 4.7 select_select_fusion
  307.6 4.0 broadcast_select_fusion.4
  312.2 41.9 %collective-permute-done.8.refs_8_ = bf16[8192,128]{1,0:T(8,128)(2,1)S(1)} collective-permute-done((bf16[8192,128]{1,0:T(8,128)(2,1)S(1)}, bf16[8192,128]{1,0:T(8,128)(2,1)S(1)}, u32[]{:S(2)}, u32[]{:S(2)}) %collective-permute-start.8) | collective-permute-done | bytes 2097184 | tf_op jit(solution)/shard_map/ppermute | solution.py:172
  354.1 41.5 %collective-permute-done.10 = bf16[8192,128]{1,0:T(8,128)(2,1)S(1)} collective-permute-done((bf16[8192,128]{1,0:T(8,128)(2,1)S(1)}, bf16[8192,128]{1,0:T(8,128)(2,1)S(1)}, u32[]{:S(2)}, u32[]{:S(2)}) %collective-permute-start.10) | collective-permute-done | bytes 2097184 | tf_op jit(solution)/shard_map/ppermute | solution.py:172
  398.9 6.4 %copy.35 = bf16[512,16,2,64]{3,1,2,0:T(8,128)(2,1)} copy(bf16[512,16,2,64]{0,2,3,1:T(2,128)(2,1)S(1)} %bitcast.48) | data formatting | bytes 4194304 | tf_op jit(solution)/shard_map/transpose | solution.py:209
  406.6 18.6 %all-gather = s32[16,64,16]{1,2,0:T(8,128)S(1)} all-gather(s32[1,64,16]{1,2,0:T(8,128)S(1)} %bitcast.51), channel_id=1, replica_groups=mesh['section'=2,'chan'=16] {'chan'}, dimensions={0}, use_global_device_ids=true | all-gather | bytes 69632 | tf_op jit(solution)/shard_map/all_gather | solution.py:248
  426.2 8.2 %stack.33 = bf16[1,64,8,2,8,2,64]{6,5,4,3,2,1,0:T(2,128)(2,1)} reshape(bf16[8192,128]{1,0:T(8,128)(2,1)} %collective-permute-done) | data formatting | bytes 4194304 | tf_op jit(solution)/shard_map/stack | solution.py:236
  434.4 5.3 copy.37
  439.8 7.3 %fusion = bf16[2,64,64,2,8,2,8]{2,6,5,0,4,1,3:T(8,128)(2,1)} fusion(bf16[1,64,8,2,8,2,64]{6,4,3,5,2,1,0:T(8,128)(2,1)} %copy.37, bf16[1,64,8,2,8,2,64]{6,4,3,5,2,1,0:T(8,128)(2,1)S(1)} %bitcast.44), kind=kLoop, calls=%fused_computation.10 | loop fusion | flops 2097152 | bytes 8388608 | tf_op jit(solution)/shard_map/transpose | solution.py:242
  447.1 9.2 %copy.38 = bf16[2,64,64,2,8,2,8]{2,6,5,4,3,1,0:T(8,128)(2,1)} copy(bf16[2,64,64,2,8,2,8]{2,6,5,0,4,1,3:T(8,128)(2,1)} %fusion) | data formatting | bytes 8388608 | tf_op jit(solution)/shard_map/transpose | solution.py:242
  456.3 8.5 %copy.41.refs_0_ = bf16[2,64,64,256]{3,2,1,0:T(8,128)(2,1)} copy(bf16[2,64,64,256]{2,3,1,0:T(8,128)(2,1)} %bitcast.45) | data formatting | bytes 8388608 | tf_op jit(solution)/shard_map/reshape | solution.py:242
  464.8 5.8 fusion.11
  470.7 7.3 %maximum_bitcast_fusion = bf16[2,64,64,2,8,2,8]{2,6,5,0,4,1,3:T(8,128)(2,1)} fusion(bf16[2,64,8,1,8,2,64]{6,4,3,5,2,1,0:T(8,128)(2,1)} %get-tuple-element.26, bf16[2,64,8,1,8,2,64]{6,4,3,5,2,1,0:T(8,128)(2,1)S(1)} %get-tuple-element.25), kind=kLoop, calls=%fused_computation.18 | loop fusion | flops 2097152 | bytes 8388608 | tf_op jit(solution)/shard_map/transpose | solution.py:242
  478.0 9.2 %copy.39 = bf16[2,64,64,2,8,2,8]{2,6,5,4,3,1,0:T(8,128)(2,1)} copy(bf16[2,64,64,2,8,2,8]{2,6,5,0,4,1,3:T(8,128)(2,1)} %maximum_bitcast_fusion) | data formatting | bytes 8388608 | tf_op jit(solution)/shard_map/transpose | solution.py:242
  487.2 8.5 %copy.42.refs_1_ = bf16[2,64,64,256]{3,2,1,0:T(8,128)(2,1)} copy(bf16[2,64,64,256]{2,3,1,0:T(8,128)(2,1)} %bitcast.46) | data formatting | bytes 8388608 | tf_op jit(solution)/shard_map/reshape | solution.py:242
  495.8 102.2 %shard_map.46 = bf16[64,51456]{1,0:T(8,128)(2,1)} custom-call(bf16[2,64,64,256]{3,2,1,0:T(8,128)(2,1)} %copy.41.refs_0_, bf16[2,64,64,256]{3,2,1,0:T(8,128)(2,1)} %copy.42.refs_1_, bf16[8192,128]{1,0:T(8,128)(2,1)} %get-tuple-element.24.refs_2_, bf16[8192,128]{1,0:T(8,128)(2,1)} %collective-permute-done.5.refs_3_, bf16[8192,128]{1,0:T(8,128)(2,1)} %copy-done.1, ...), custom_call_target="tpu_custom_call" | custom-call | tf_op jit(solution)/shard_map/pallas_call | solution.py:151
  (80 shorter events, 42.6 us)
Async XLA Ops:
  0.1 34.7 %copy-start.6 = (s32[8]{0:T(128)S(1)}, s32[8]{0:T(128)}, u32[]{:S(2)}) copy-start(s32[8]{0:T(128)} %param.5) | copy-start | bytes 100
  34.8 29.9 %copy-start.5 = (s32[16,64]{1,0:T(8,128)S(1)}, s32[16,64]{1,0:T(8,128)}, u32[]{:S(2)}) copy-start(s32[16,64]{1,0:T(8,128)} %param.6) | copy-start | bytes 12292
  64.8 3.5 copy-start.4
  104.0 50.9 %collective-permute-start.1 = (bf16[8192,128]{1,0:T(8,128)(2,1)}, bf16[8192,128]{1,0:T(8,128)(2,1)}, u32[]{:S(2)}, u32[]{:S(2)}) collective-permute-start(bf16[8192,128]{1,0:T(8,128)(2,1)} %reshape.175), channel_id=1, source_target_pairs={{4,0},{5,1},{6,2},{7,3},{8,4},{9,5},{10,6},{11,7},{12,8},{13,9},{1... | collective-permute-start | bytes 6291464 | tf_op jit(solution)/shard_map/ppermute | solution.py:176
  154.9 49.0 %collective-permute-start.3 = (bf16[8192,128]{1,0:T(8,128)(2,1)}, bf16[8192,128]{1,0:T(8,128)(2,1)}, u32[]{:S(2)}, u32[]{:S(2)}) collective-permute-start(bf16[8192,128]{1,0:T(8,128)(2,1)} %collective-permute-done.1), channel_id=1, source_target_pairs={{4,0},{5,1},{6,2},{7,3},{8,4},{9,5},{10,6},{11,7},{12,8},{13,9},{1... | collective-permute-start | bytes 6291464 | tf_op jit(solution)/shard_map/ppermute | solution.py:176
  209.7 48.8 %collective-permute-start.2 = (bf16[8192,128]{1,0:T(8,128)(2,1)}, bf16[8192,128]{1,0:T(8,128)(2,1)}, u32[]{:S(2)}, u32[]{:S(2)}) collective-permute-start(bf16[8192,128]{1,0:T(8,128)(2,1)} %get-tuple-element.32), channel_id=1, source_target_pairs={{0,2},{1,3},{2,0},{3,1},{4,6},{5,7},{6,4},{7,5},{8,10},{9,11},{10,... | collective-permute-start | bytes 6291464 | tf_op jit(solution)/shard_map/ppermute | solution.py:176
  210.5 90.4 %collective-permute-start.4 = (bf16[8192,128]{1,0:T(8,128)(2,1)}, bf16[8192,128]{1,0:T(8,128)(2,1)}, u32[]{:S(2)}, u32[]{:S(2)}) collective-permute-start(bf16[8192,128]{1,0:T(8,128)(2,1)} %get-tuple-element.35), channel_id=1, source_target_pairs={{0,2},{1,3},{2,0},{3,1},{4,6},{5,7},{6,4},{7,5},{8,10},{9,11},{10,... | collective-permute-start | bytes 6291464 | tf_op jit(solution)/shard_map/ppermute | solution.py:176
  211.8 214.5 %collective-permute-start = (bf16[8192,128]{1,0:T(8,128)(2,1)}, bf16[8192,128]{1,0:T(8,128)(2,1)}, u32[]{:S(2)}, u32[]{:S(2)}) collective-permute-start(bf16[8192,128]{1,0:T(8,128)(2,1)} %reshape.175), channel_id=1, source_target_pairs={{0,16},{16,0},{1,17},{17,1},{2,18},{18,2},{3,19},{19,3},{4,20},{20... | collective-permute-start | bytes 6291464 | tf_op jit(solution)/shard_map/ppermute | solution.py:172
  217.8 93.9 %collective-permute-start.7 = (bf16[8192,128]{1,0:T(8,128)(2,1)}, bf16[8192,128]{1,0:T(8,128)(2,1)S(1)}, u32[]{:S(2)}, u32[]{:S(2)}) collective-permute-start(bf16[8192,128]{1,0:T(8,128)(2,1)} %get-tuple-element.31), channel_id=1, source_target_pairs={{0,16},{16,0},{1,17},{17,1},{2,18},{18,2},{3,19},{19,3},{4,20},{20... | collective-permute-start | bytes 6291464 | tf_op jit(solution)/shard_map/ppermute | solution.py:172
  305.6 6.1 %copy-start.1 = (bf16[8192,128]{1,0:T(8,128)(2,1)}, bf16[8192,128]{1,0:T(8,128)(2,1)S(1)}, u32[]{:S(2)}) copy-start(bf16[8192,128]{1,0:T(8,128)(2,1)S(1)} %get-tuple-element.22.refs_4_) | copy-start | bytes 6291460
  305.6 48.5 %collective-permute-start.8 = (bf16[8192,128]{1,0:T(8,128)(2,1)S(1)}, bf16[8192,128]{1,0:T(8,128)(2,1)S(1)}, u32[]{:S(2)}, u32[]{:S(2)}) collective-permute-start(bf16[8192,128]{1,0:T(8,128)(2,1)S(1)} %get-tuple-element.30), channel_id=1, source_target_pairs={{0,16},{16,0},{1,17},{17,1},{2,18},{18,2},{3,19},{19,3},{4,20},{20... | collective-permute-start | bytes 6291464 | tf_op jit(solution)/shard_map/ppermute | solution.py:172
  306.7 88.9 %collective-permute-start.10 = (bf16[8192,128]{1,0:T(8,128)(2,1)S(1)}, bf16[8192,128]{1,0:T(8,128)(2,1)S(1)}, u32[]{:S(2)}, u32[]{:S(2)}) collective-permute-start(bf16[8192,128]{1,0:T(8,128)(2,1)S(1)} %get-tuple-element.29), channel_id=1, source_target_pairs={{0,16},{16,0},{1,17},{17,1},{2,18},{18,2},{3,19},{19,3},{4,20},{20... | collective-permute-start | bytes 6291464 | tf_op jit(solution)/shard_map/ppermute | solution.py:172
  311.7 184.1 %collective-permute-start.5 = (bf16[8192,128]{1,0:T(8,128)(2,1)}, bf16[8192,128]{1,0:T(8,128)(2,1)}, u32[]{:S(2)}, u32[]{:S(2)}) collective-permute-start(bf16[8192,128]{1,0:T(8,128)(2,1)} %get-tuple-element.23), channel_id=1, source_target_pairs={{0,1},{1,0},{2,3},{3,2},{4,5},{5,4},{6,7},{7,6},{8,9},{9,8},{10,11... | collective-permute-start | bytes 6291464 | tf_op jit(solution)/shard_map/ppermute | solution.py:176
  311.7 86.3 %copy-start.2 = (bf16[8192,128]{1,0:T(8,128)(2,1)}, bf16[8192,128]{1,0:T(8,128)(2,1)S(1)}, u32[]{:S(2)}) copy-start(bf16[8192,128]{1,0:T(8,128)(2,1)S(1)} %collective-permute-done.7.refs_6_) | copy-start | bytes 6291460
  311.7 184.1 %collective-permute-start.6 = (bf16[8192,128]{1,0:T(8,128)(2,1)}, bf16[8192,128]{1,0:T(8,128)(2,1)}, u32[]{:S(2)}, u32[]{:S(2)}) collective-permute-start(bf16[8192,128]{1,0:T(8,128)(2,1)} %get-tuple-element.21), channel_id=1, source_target_pairs={{0,1},{1,0},{2,3},{3,2},{4,5},{5,4},{6,7},{7,6},{8,9},{9,8},{10,11... | collective-permute-start | bytes 6291464 | tf_op jit(solution)/shard_map/ppermute | solution.py:176
  354.1 43.9 %copy-start.3 = (bf16[8192,128]{1,0:T(8,128)(2,1)}, bf16[8192,128]{1,0:T(8,128)(2,1)S(1)}, u32[]{:S(2)}) copy-start(bf16[8192,128]{1,0:T(8,128)(2,1)S(1)} %collective-permute-done.8.refs_8_) | copy-start | bytes 6291460
  398.0 97.7 %collective-permute-start.9 = (bf16[8192,128]{1,0:T(8,128)(2,1)}, bf16[8192,128]{1,0:T(8,128)(2,1)}, u32[]{:S(2)}, u32[]{:S(2)}) collective-permute-start(bf16[8192,128]{1,0:T(8,128)(2,1)} %get-tuple-element.34), channel_id=1, source_target_pairs={{0,1},{1,0},{2,3},{3,2},{4,5},{5,4},{6,7},{7,6},{8,9},{9,8},{10,11... | collective-permute-start | bytes 6291464 | tf_op jit(solution)/shard_map/ppermute | solution.py:176
  398.0 97.7 %collective-permute-start.11 = (bf16[8192,128]{1,0:T(8,128)(2,1)}, bf16[8192,128]{1,0:T(8,128)(2,1)}, u32[]{:S(2)}, u32[]{:S(2)}) collective-permute-start(bf16[8192,128]{1,0:T(8,128)(2,1)} %get-tuple-element.33), channel_id=1, source_target_pairs={{0,1},{1,0},{2,3},{3,2},{4,5},{5,4},{6,7},{7,6},{8,9},{9,8},{10,11... | collective-permute-start | bytes 6291464 | tf_op jit(solution)/shard_map/ppermute | solution.py:176
  398.9 26.5 %copy-start.7 = (s32[64]{0:T(128)S(1)}, s32[64]{0:T(128)}, u32[]{:S(2)}) copy-start(s32[64]{0:T(128)} %param.7) | copy-start | bytes 772
  434.4 5.3 copy-start
